TPU v7x, 512 devices: a whole 4x8x8 slice. The times are simulated.
512 devices in a mesh: seq: 64 (over z_hi, y, x), mp: 8 (over z_lo, core).
Axes of the slice: x: 4, y: 8, z: 8 (z_hi: 2, z_lo: 4; z = z_hi * 4 + z_lo), core: 2. Of those that a mesh axis runs over, the one named last changes fastest.
Arguments:
- stream_q: bfloat16 [16384, 2048], P('seq', 'mp'), may hold values from -6 to 6
- stream_k: bfloat16 [16384, 2048], P('seq', 'mp'), may hold values from -6 to 6
- stream_v: bfloat16 [16384, 2048], P('seq', 'mp'), may hold values from -6 to 6
- filter_taps: float32 [2048, 128], P('mp'), may hold values from -4 to 4
- decay_rate: float32 [2048], P('mp'), may hold values from 0.004 to 0.15
- residual: bfloat16 [16384, 2048], P('seq', 'mp'), may hold values from -6 to 6
- norm_gain: float32 [2048], P('mp'), may hold values from 0.5 to 1.5
- queries: bfloat16 [16384, 2048], P('seq', 'mp'), may hold values from -50 to 50
- keys: bfloat16 [16384, 2048], P('seq', 'mp'), may hold values from -6 to 6
Outputs:
- normed: bfloat16 [16384, 2048], P('seq', 'mp')
- attended: bfloat16 [16384, 2048], P('seq', 'mp')
All inputs are finite; a program needn't handle non-finite values.
Results may differ from a plain program's by a relative error of at most 0.0061.
Values may be sent and summed in bfloat16 or wider, within the bound.
A program may use at most 128 MiB of HBM per device.

v0:
```python
import math

import jax
import jax.numpy as jnp
from jax import lax
from jax.sharding import PartitionSpec as P

CH = 2048
HD = 128


norm_eps = 1e-06
neg_large = -1e30


def passed_along(value, axis, steps):
    count = lax.axis_size(axis)
    first, last = (max(0, -steps), min(count, count - steps))
    return lax.ppermute(value, axis, [(source, source + steps) for source in range(first, last)])


def causal_filter(extended, kernel):
    tap_count = kernel.shape[1]
    row_count = extended.shape[0] - (tap_count - 1)
    total = extended[tap_count - 1 : tap_count - 1 + row_count] * kernel[:, 0][None, :]
    for tap in range(1, tap_count):
        start = tap_count - 1 - tap
        total = total + extended[start : start + row_count] * kernel[:, tap][None, :]
    return total


def attend_block(carried, query_heads, query_pos, key_part, value_part, key_start, score_scale):
    numerator, running_max, denominator = carried
    score = (
        jnp.einsum("qhd,khd->hqk", query_heads, key_part, preferred_element_type=jnp.float32)
        * score_scale
    )
    key_pos = key_start + jnp.arange(key_part.shape[0], dtype=jnp.int32)
    visible = key_pos[None, None, :] <= query_pos[None, :, None]
    score = jnp.where(visible, score, neg_large)
    new_max = jnp.maximum(running_max, jnp.max(score, axis=2))
    weight = jnp.where(visible, jnp.exp(score - new_max[..., None]), 0.0)
    factor = jnp.exp(running_max - new_max)
    denominator = denominator * factor + jnp.sum(weight, axis=2)
    numerator = numerator * factor[..., None] + jnp.einsum(
        "hqk,khd->hqd", weight.astype(jnp.bfloat16), value_part, preferred_element_type=jnp.float32
    )
    return (numerator, new_max, denominator)


def attention(query_rows, query_pos, keys, normed, head_count):
    query_count = query_rows.shape[0]
    query_heads = query_rows.reshape(query_count, head_count, HD)
    score_scale = 1.0 / math.sqrt(HD)
    initial = (
        jnp.zeros((head_count, query_count, HD), jnp.float32),
        jnp.full((head_count, query_count), neg_large, jnp.float32),
        jnp.zeros((head_count, query_count), jnp.float32),
    )
    key_piece = lax.all_gather(keys, "seq", axis=0, tiled=True)
    value_piece = lax.all_gather(normed, "seq", axis=0, tiled=True)
    key_count = key_piece.shape[0]
    key_heads = key_piece.reshape(key_count, head_count, HD)
    value_heads = value_piece.reshape(key_count, head_count, HD)
    block_width = math.gcd(key_count, 512)

    def block_step(step_index, inner):
        offset = step_index * block_width
        key_part = lax.dynamic_slice_in_dim(key_heads, offset, block_width, 0)
        value_part = lax.dynamic_slice_in_dim(value_heads, offset, block_width, 0)
        return attend_block(
            inner, query_heads, query_pos, key_part, value_part, offset, score_scale
        )

    numerator, running_max, denominator = lax.fori_loop(
        0, key_count // block_width, block_step, initial
    )
    result = numerator / denominator[..., None]
    return result.transpose(1, 0, 2).reshape(query_count, head_count * HD).astype(jnp.bfloat16)


def local(
    stream_q, stream_k, stream_v, filter_taps, decay_rate, residual, norm_gain, queries, keys
):
    row_count, chan_local = stream_q.shape
    tap_count = filter_taps.shape[1]
    gated_input = (stream_k.astype(jnp.float32) * stream_v.astype(jnp.float32)).astype(jnp.bfloat16)
    rim_rows = passed_along(gated_input[row_count - (tap_count - 1) :], "seq", 1)
    extended = jnp.concatenate([rim_rows, gated_input], axis=0).astype(jnp.float32)
    tap_index = jnp.arange(tap_count).astype(jnp.float32)
    kernel = filter_taps * jnp.exp(-decay_rate[:, None] * tap_index[None, :])
    filtered = causal_filter(extended, kernel)
    hyena_out = (stream_q.astype(jnp.float32) * filtered).astype(jnp.bfloat16)
    summed = residual.astype(jnp.float32) + hyena_out.astype(jnp.float32)
    square_total = lax.psum(jnp.sum(summed * summed, axis=1), "mp")
    inverse_rms = lax.rsqrt(square_total / CH + norm_eps)
    normed = (summed * inverse_rms[:, None] * norm_gain[None, :]).astype(jnp.bfloat16)
    head_count = chan_local // HD
    own_pos = lax.axis_index("seq") * row_count + jnp.arange(row_count, dtype=jnp.int32)
    attended = attention(queries, own_pos, keys, normed, head_count)
    return (normed, attended)


def solution(mesh):
    in_specs = (
        P("seq", "mp"),
        P("seq", "mp"),
        P("seq", "mp"),
        P("mp", None),
        P("mp"),
        P("seq", "mp"),
        P("mp"),
        P("seq", "mp"),
        P("seq", "mp"),
    )
    out_specs = (P("seq", "mp"), P("seq", "mp"))
    return jax.shard_map(local, mesh=mesh, in_specs=in_specs, out_specs=out_specs, check_vma=False)
```

profile of v0, /device:TPU:1, one launch (start us, length us, event | category | flops | bytes accessed | tf_op | source)
XLA Modules:
  0.0 597.0 jit_solution(13176938043259709506)
XLA Ops:
  8.2 3.9 collective-permute-start
  13.9 1.4 slice_reduce_fusion.127
  15.3 1.4 slice_reduce_fusion.126
  16.7 1.4 slice_reduce_fusion.125
  18.1 1.4 slice_reduce_fusion.124
  19.5 1.4 slice_reduce_fusion.123
  20.9 1.4 slice_reduce_fusion.122
  23.5 6.5 %multiply_reduce_fusion = (f32[256]{0:T(256)S(1)}, bf16[256,256]{1,0:T(8,128)(2,1)S(1)}) fusion(bf16[256,256]{1,0:T(8,128)(2,1)S(1)} %copy-done, f32[256]{0:T(256)S(1)} %get-tuple-element.191, f32[383,256]{1,0:T(8,128)S(1)} %maximum_convert_fusion, f32[256]{0:T(256)S(1)} %get-tuple-element.192, f32[256]{0:T(256)S(1)} %get-tuple-element.193, ...), kind=kLoop, calls=%fused_computation.284 | loop fusion | flops 17235712 | bytes 34079744 | tf_op jit(solution)/shard_map/reduce_sum | solution.py:95
  30.0 17.1 %psum.7 = f32[256]{0:T(256)S(1)} all-reduce(f32[256]{0:T(256)S(1)} %get-tuple-element.336), channel_id=1, replica_groups=mesh['seq'=64,'mp'=8] {'mp'}, use_global_device_ids=true, to_apply=%region_1.0 | all-reduce | flops 256 | bytes 2048 | tf_op jit(solution)/shard_map/psum | solution.py:95
  49.1 199.0 %all-gather.5.cloned.1.call-done = bf16[16384,256]{1,0:T(8,128)(2,1)} async-done(((bf16[256,256]{1,0:T(8,128)(2,1)}), bf16[16384,256]{1,0:T(8,128)(2,1)}) %all-gather.5.cloned.1.call-update) | async-done | bytes 8388624 | tf_op jit(solution)/shard_map/all_gather | solution.py:61
  248.1 12.5 %reshape.193 = bf16[16384,2,128]{2,1,0:T(2,128)(2,1)} reshape(bf16[16384,256]{1,0:T(8,128)(2,1)} %all-gather.5.cloned.1.call-done) | data formatting | bytes 16777216 | tf_op jit(solution)/shard_map/reshape | solution.py:64
  260.7 217.4 %all-gather.3.cloned.1.call-done = bf16[16384,256]{0,1:T(8,128)(2,1)} async-done(((bf16[256,256]{0,1:T(8,128)(2,1)}), bf16[16384,256]{0,1:T(8,128)(2,1)}) %all-gather.3.cloned.1.call-update) | async-done | bytes 8388624 | tf_op jit(solution)/shard_map/all_gather | solution.py:60
  478.1 111.3 %while.18 = (s32[]{:T(128)}, f32[2,256,128]{2,1,0:T(8,128)S(1)}, f32[2,256]{1,0:T(2,128)S(1)}, f32[2,256]{1,0:T(2,128)S(1)}, bf16[16384,2,128]{0,2,1:T(8,128)(2,...) while((s32[]{:T(128)}, f32[2,256,128]{2,1,0:T(8,128)S(1)}, ...), condition=%wide.region_5.6_spmd.clone, body=%wide.region_2.5_spmd.clone.sunk | while | flops 136908032 | bytes 5413055 | solution.py:75
  478.2 1.3 fusion.160
  481.7 1.3 fusion.160
  485.2 1.3 fusion.160
  488.7 1.3 fusion.160
  492.1 1.3 fusion.160
  495.6 1.3 fusion.160
  499.1 1.3 fusion.160
  506.1 1.3 fusion.160
  509.5 1.3 fusion.160
  520.0 1.3 fusion.160
  523.5 1.3 fusion.160
  533.9 1.3 fusion.160
  537.4 1.3 fusion.160
  547.8 1.3 fusion.160
  551.3 1.3 fusion.160
  561.7 1.3 fusion.160
  565.2 1.3 fusion.160
  575.7 1.3 fusion.160
  579.1 1.3 fusion.160
  (332 shorter events, 90.1 us)
Async XLA Ops:
  7.2 241.0 %all-gather.5.cloned.1.call-start = ((), (), s32[]{:S(2)}) async-start(), calls=%async_computation.1 | async-start | bytes 8519680 | tf_op jit(solution)/shard_map/all_gather | solution.py:61
  8.2 15.2 %collective-permute-start = (bf16[127,256]{1,0:T(8,128)(2,1)S(1)}, bf16[127,256]{1,0:T(8,128)(2,1)S(1)}, u32[]{:S(2)}, u32[]{:S(2)}) collective-permute-start(bf16[127,256]{1,0:T(8,128)(2,1)S(1)} %slice.1028), channel_id=1, source_target_pairs={{0,8},{8,16},{16,24},{24,32},{32,40},{40,48},{48,56},{56,64},{64,7... | collective-permute-start | bytes 195080 | tf_op jit(solution)/shard_map/ppermute | solution.py:19
  13.9 9.6 %copy-start = (bf16[256,256]{1,0:T(8,128)(2,1)S(1)}, bf16[256,256]{1,0:T(8,128)(2,1)}, u32[]{:S(2)}) copy-start(bf16[256,256]{1,0:T(8,128)(2,1)} %param.16) | copy-start | bytes 393220
  13.9 9.6 %copy-start.1 = (bf16[256,256]{1,0:T(8,128)(2,1)S(1)}, bf16[256,256]{1,0:T(8,128)(2,1)}, u32[]{:S(2)}) copy-start(bf16[256,256]{1,0:T(8,128)(2,1)} %param.11) | copy-start | bytes 393220
  23.5 23.7 %copy-start.4 = (f32[256]{0:T(256)S(1)}, f32[256]{0:T(256)}, u32[]{:S(2)}) copy-start(f32[256]{0:T(256)} %param.17) | copy-start | bytes 3076
  23.5 24.5 %copy-start.2 = (bf16[256,256]{1,0:T(8,128)(2,1)S(1)}, bf16[256,256]{1,0:T(8,128)(2,1)}, u32[]{:S(2)}) copy-start(bf16[256,256]{1,0:T(8,128)(2,1)} %param.19) | copy-start | bytes 393220
  23.5 25.3 %copy-start.3 = (bf16[256,256]{1,0:T(8,128)(2,1)S(1)}, bf16[256,256]{1,0:T(8,128)(2,1)}, u32[]{:S(2)}) copy-start(bf16[256,256]{1,0:T(8,128)(2,1)} %param.18) | copy-start | bytes 393220
  48.0 430.1 %all-gather.3.cloned.1.call-start = ((), (), s32[]{:S(2)}) async-start(), calls=%async_computation | async-start | bytes 8519680 | tf_op jit(solution)/shard_map/all_gather | solution.py:60
Sparse Core Ops, SparseCore 0:
  48.1 199.9 all-gather.4
  253.0 224.9 all-gather.2
where the time goes:
time: 604 us; the launch traced here: 597 us
  waiting for transfers between devices  416 us (69%)
  local copies, waits for them, and re-layouts  59.6 us (10%)
  matrix products  59.5 us (10%)
  other arithmetic  23.6 us (4%)
  blocking collectives  17.1 us (3%)
  between operations  14.2 us (2%)
    all_gather x1, waiting for transfers between devices, attention(): key_piece = lax.all_gather(keys, 'seq', axis=0, tiled=True)  217 us
    all_gather x1, waiting for transfers between devices, attention(): value_piece = lax.all_gather(normed, 'seq', axis=0, tiled=True)  199 us
    dot_general x32, matrix products, attend_block(): jnp.einsum('qhd,khd->hqk', query_heads, key_part, preferred_element_type=...  42.4 us
    dynamic_slice x32, local copies, waits for them, and re-layouts, block_step(): value_part = lax.dynamic_slice_in_dim(value_heads, offset, block_width, 0)  36.4 us
    psum x1, blocking collectives, local(): square_total = lax.psum(jnp.sum(summed * summed, axis=1), 'mp')  17.1 us
    dot_general x32, matrix products, attend_block(): jnp.einsum('hqk,khd->hqd', weight.astype(jnp.bfloat16), value_part, prefe...  17.1 us
    reshape x1, local copies, waits for them, and re-layouts, attention(): value_heads = value_piece.reshape(key_count, head_count, HD)  12.5 us
  transfers between devices with their start and end apart: 3, of which 2 were waited for; matrix products, arithmetic and copies ran while one was open for 4% of the time, Pallas kernels for 0%

commit v1 on v0

v1 whole, which is shorter than its diff:
```python
import functools
import math

import jax
import jax.numpy as jnp
from jax import lax
from jax.experimental import pallas as pl
from jax.experimental.pallas import tpu as pltpu
from jax.sharding import Mesh, PartitionSpec as P

HD = 128
ROWS = 256
WIDTH = 256
TAPS = 128
HEADS = WIDTH // HD
EPS = 1e-06
LOW = -1e30
SCALE2 = math.log2(math.e) / math.sqrt(HD)
MESH = pl.DeviceIdType.MESH
AXES = ("zh", "y", "x", "mp")


def body(
    sizes,
    sq_ref, sk_ref, sv_ref, taps_ref, decay_ref, res_ref, gain_ref, q_ref, k_ref,
    normed_ref, out_ref,
    halo_k, halo_v, shifted, taps_t, filtered, squares,
    q_all, k_all, v_all, part, part_in, stat, stat_in, m_ref, l_ref, acc_ref,
    halo_send, halo_recv, sq_send, sq_recv, q_send, q_recv,
    k_send, k_recv, v_send, v_recv, p_send, p_recv, s_send, s_recv,
):
    nz, ny, nx, nm = sizes
    zh, y, x, mp = (lax.axis_index(name) for name in AXES)
    seq = (zh * ny + y) * nx + x
    mine = zh * nx + x
    other = (1 - zh) * nx + x
    total_seq = nz * ny * nx

    def at_seq(s):
        return (s // (ny * nx), lax.rem(s // nx, ny), lax.rem(s, nx), mp)

    def at_y(p):
        return (zh, p, x, mp)

    def at_x(p):
        return (zh, y, p, mp)

    def at_mp(p):
        return (zh, y, x, p)

    partner = (1 - zh, y, x, mp)
    following = at_seq(lax.rem(seq + 1, total_seq))
    previous = at_seq(lax.rem(seq + total_seq - 1, total_seq))

    def remote(src, dst, send, recv, device):
        return pltpu.make_async_remote_copy(
            src_ref=src, dst_ref=dst, send_sem=send, recv_sem=recv,
            device_id=device, device_id_type=MESH,
        )

    barrier = pltpu.get_barrier_semaphore()
    greeted = [previous, partner]
    greeted += [at_y(lax.rem(y + d, ny)) for d in range(1, ny)]
    greeted += [at_x(lax.rem(x + d, nx)) for d in range(1, nx)]
    greeted += [at_mp(lax.rem(mp + d, nm)) for d in range(1, nm)]
    for device in greeted:
        pl.semaphore_signal(barrier, inc=1, device_id=device, device_id_type=MESH)
    pl.semaphore_wait(barrier, len(greeted))

    tail = pl.ds(ROWS - TAPS, TAPS)
    halos = [
        remote(sk_ref.at[tail], halo_k, halo_send.at[0], halo_recv.at[0], following),
        remote(sv_ref.at[tail], halo_v, halo_send.at[1], halo_recv.at[1], following),
    ]
    for copy in halos:
        copy.start()

    sends = []

    def spread(src, table, send, recv, first, slot):
        for d in range(1, nx):
            copy = remote(
                src, table.at[slot], send.at[first + d], recv.at[slot],
                at_x(lax.rem(x + d, nx)),
            )
            copy.start()
            sends.append(copy)

    def across(src, table, send, recv):
        copy = remote(src, table.at[mine], send.at[0], recv.at[mine], partner)
        copy.start()
        sends.append(copy)

    def arrived(table, send, recv, slot):
        remote(table.at[slot], table.at[slot], send.at[0], recv.at[slot], partner).wait_recv()

    across(k_ref, k_all, k_send, k_recv)
    spread(k_ref, k_all, k_send, k_recv, 0, mine)
    for d in range(1, ny):
        copy = remote(
            q_ref, q_all.at[y], q_send.at[d], q_recv.at[y], at_y(lax.rem(y + d, ny))
        )
        copy.start()
        sends.append(copy)
    q_all[y] = q_ref[...]
    k_all[mine] = k_ref[...]

    steps = lax.broadcasted_iota(jnp.int32, (TAPS, WIDTH), 0).astype(jnp.float32)
    taps_t[...] = taps_ref[...].T * jnp.exp(-decay_ref[...] * steps)

    def gate(a, b):
        return (a.astype(jnp.float32) * b.astype(jnp.float32)).astype(jnp.bfloat16).astype(jnp.float32)

    own_gated = gate(sk_ref[...], sv_ref[...])
    for r in range(8):
        shifted[r, TAPS + r : TAPS + r + ROWS, :] = own_gated
    for copy in halos:
        copy.wait()
    edge = gate(halo_k[...], halo_v[...])
    edge = jnp.where(seq > 0, edge, 0.0)
    for r in range(8):
        shifted[r, r : r + TAPS, :] = edge

    arrived(k_all, k_send, k_recv, other)
    spread(k_all.at[other], k_all, k_send, k_recv, nx - 1, other)

    chunk = 64

    def filter_chunk(c, _):
        base = TAPS + c * chunk

        def eight(j, total):
            coeff = taps_t[pl.ds(pl.multiple_of(j * 8, 8), 8), :]
            rows = pl.ds(pl.multiple_of(base - j * 8, 8), chunk)
            for r in range(8):
                total = total + shifted[r, rows, :] * coeff[r : r + 1, :]
            return total

        total = lax.fori_loop(0, TAPS // 8, eight, jnp.zeros((chunk, WIDTH), jnp.float32))
        here = pl.ds(pl.multiple_of(c * chunk, chunk), chunk)
        hyena = (sq_ref[here, :].astype(jnp.float32) * total).astype(jnp.bfloat16)
        filtered[here, :] = res_ref[here, :].astype(jnp.float32) + hyena.astype(jnp.float32)
        return 0

    lax.fori_loop(0, ROWS // chunk, filter_chunk, 0)
    summed = filtered[...]
    own_square = jnp.sum(summed * summed, axis=1, keepdims=True)
    squares[mp] = jnp.broadcast_to(own_square, (ROWS, 128)).T[:8]
    for d in range(1, nm):
        copy = remote(
            squares.at[mp], squares.at[mp], sq_send.at[d], sq_recv.at[mp],
            at_mp(lax.rem(mp + d, nm)),
        )
        copy.start()
        sends.append(copy)
    for d in range(1, nm):
        source = lax.rem(mp + d, nm)
        remote(
            squares.at[source], squares.at[source], sq_send.at[d], sq_recv.at[source],
            at_mp(source),
        ).wait_recv()
    square = squares[0]
    for i in range(1, nm):
        square = square + squares[i]
    inverse = lax.rsqrt(square / (nm * WIDTH) + EPS)
    inverse = jnp.concatenate([inverse] * 16, axis=0).T
    inverse = jnp.concatenate([inverse] * (WIDTH // 128), axis=1)
    normed = (filtered[...] * inverse * gain_ref[...]).astype(jnp.bfloat16)
    normed_ref[...] = normed
    v_all[mine] = normed
    across(v_all.at[mine], v_all, v_send, v_recv)
    spread(v_all.at[mine], v_all, v_send, v_recv, 0, mine)
    arrived(v_all, v_send, v_recv, other)
    spread(v_all.at[other], v_all, v_send, v_recv, nx - 1, other)
    for d in range(1, ny):
        source = lax.rem(y + d, ny)
        remote(
            q_all.at[source], q_all.at[source], q_send.at[d], q_recv.at[source], at_y(source)
        ).wait_recv()
    for d in range(1, nx):
        column = lax.rem(x + d, nx)
        for z in range(nz):
            arrived(k_all, k_send, k_recv, z * nx + column)
            arrived(v_all, v_send, v_recv, z * nx + column)

    def tile(h, q_slot, slot, masked):
        lanes = slice(h * HD, (h + 1) * HD)
        score = lax.dot_general(
            q_all[q_slot, :, lanes], k_all[slot, :, lanes], (((1,), (1,)), ((), ())),
            preferred_element_type=jnp.float32,
        ) * SCALE2
        if masked:
            row = lax.broadcasted_iota(jnp.int32, (ROWS, ROWS), 0)
            col = lax.broadcasted_iota(jnp.int32, (ROWS, ROWS), 1)
            score = jnp.where(col <= row, score, LOW)
        before = m_ref[h]
        now = jnp.maximum(before, jnp.max(score, axis=1, keepdims=True))
        m_ref[h] = now
        weight = jnp.exp2(score - jnp.concatenate([now] * (ROWS // 128), axis=1))
        if masked:
            weight = jnp.where(col <= row, weight, 0.0)
        factor = jnp.exp2(before - now)
        lane_sum = weight[:, :128]
        for i in range(1, ROWS // 128):
            lane_sum = lane_sum + weight[:, i * 128 : (i + 1) * 128]
        l_ref[h] = l_ref[h] * factor + lane_sum
        acc_ref[h] = acc_ref[h] * factor + jnp.dot(
            weight.astype(jnp.bfloat16), v_all[slot, :, lanes],
            preferred_element_type=jnp.float32,
        )

    def query_block(i, _):
        q_slot = lax.rem(y + 1 + i, ny)
        is_own = i == ny - 1
        m_ref[...] = jnp.full_like(m_ref, LOW)
        l_ref[...] = jnp.zeros_like(l_ref)
        acc_ref[...] = jnp.zeros_like(acc_ref)
        inside = jnp.where(q_slot > y, nx, jnp.where(is_own, x, 0))
        count = zh * nx + inside

        def step(slot, carry):
            for h in range(HEADS):
                tile(h, q_slot, slot, False)
            return carry

        lax.fori_loop(0, count, step, 0)

        @pl.when(is_own)
        def _():
            for h in range(HEADS):
                tile(h, q_slot, mine, True)

        logs = []
        for h in range(HEADS):
            amount = jnp.sum(l_ref[h], axis=1, keepdims=True)
            amount = jnp.where(amount > 0.0, amount, 1.0)
            part[q_slot, :, h * HD : (h + 1) * HD] = (acc_ref[h] / amount).astype(jnp.bfloat16)
            logs.append(m_ref[h] + jnp.log2(amount))
        lane = lax.broadcasted_iota(jnp.int32, (ROWS, 128), 1)
        stat[q_slot] = jnp.where(lane == 0, logs[0], logs[1]).T[:8]

        @pl.when(jnp.logical_not(is_own))
        def _():
            remote(
                part.at[q_slot], part_in.at[y], p_send.at[q_slot], p_recv.at[y], at_y(q_slot)
            ).start()
            remote(
                stat.at[q_slot], stat_in.at[y], s_send.at[q_slot], s_recv.at[y], at_y(q_slot)
            ).start()

        return 0

    lax.fori_loop(0, ny, query_block, 0)

    for d in range(1, ny):
        source = lax.rem(y + d, ny)
        last = remote(
            part.at[source], part_in.at[source], p_send.at[source], p_recv.at[source],
            at_y(source),
        )
        last.wait()
        last = remote(
            stat.at[source], stat_in.at[source], s_send.at[source], s_recv.at[source],
            at_y(source),
        )
        last.wait()

    stats = [stat[y]] + [stat_in[lax.rem(y + d, ny)] for d in range(1, ny)]
    top = functools.reduce(jnp.maximum, stats)
    raised = [jnp.exp2(s - top) for s in stats]
    norm = functools.reduce(jnp.add, raised)
    share = jnp.concatenate([e / norm for e in raised], axis=0)
    if ny < 16:
        share = jnp.concatenate([share, jnp.zeros((128 - 8 * ny, ROWS), jnp.float32)], axis=0)
    share = share.T
    for h in range(HEADS):
        lanes = slice(h * HD, (h + 1) * HD)
        total = share[:, h : h + 1] * part[y, :, lanes].astype(jnp.float32)
        for d in range(1, ny):
            piece = part_in[lax.rem(y + d, ny), :, lanes].astype(jnp.float32)
            total = total + share[:, d * 8 + h : d * 8 + h + 1] * piece
        out_ref[:, lanes] = total.astype(jnp.bfloat16)

    for copy in sends:
        copy.wait_send()


def build(mesh, sizes):
    nz, ny, nx, nm = sizes
    group = nz * nx

    def local(stream_q, stream_k, stream_v, taps, decay, residual, gain, queries, keys):
        block = jax.ShapeDtypeStruct((ROWS, WIDTH), jnp.bfloat16)
        bf, f32 = jnp.bfloat16, jnp.float32
        vmem = pltpu.VMEM
        dma = pltpu.SemaphoreType.DMA
        return pl.pallas_call(
            functools.partial(body, sizes),
            out_shape=(block, block),
            in_specs=[pl.BlockSpec(memory_space=pltpu.VMEM)] * 9,
            out_specs=(pl.BlockSpec(memory_space=pltpu.VMEM),) * 2,
            scratch_shapes=[
                vmem((TAPS, WIDTH), bf), vmem((TAPS, WIDTH), bf),
                vmem((8, TAPS + ROWS + 8, WIDTH), f32), vmem((TAPS, WIDTH), f32),
                vmem((ROWS, WIDTH), f32), vmem((nm, 8, ROWS), f32),
                vmem((ny, ROWS, WIDTH), bf), vmem((group, ROWS, WIDTH), bf),
                vmem((group, ROWS, WIDTH), bf), vmem((ny, ROWS, WIDTH), bf),
                vmem((ny, ROWS, WIDTH), bf), vmem((ny, 8, ROWS), f32), vmem((ny, 8, ROWS), f32),
                vmem((HEADS, ROWS, 128), f32), vmem((HEADS, ROWS, 128), f32),
                vmem((HEADS, ROWS, HD), f32),
                dma((2,)), dma((2,)), dma((nm,)), dma((nm,)), dma((ny,)), dma((ny,)),
                dma((2 * nx,)), dma((group,)), dma((2 * nx,)), dma((group,)),
                dma((ny,)), dma((ny,)), dma((ny,)), dma((ny,)),
            ],
            compiler_params=pltpu.CompilerParams(
                collective_id=0, has_side_effects=True, vmem_limit_bytes=60 * 1024 * 1024
            ),
        )(
            stream_q, stream_k, stream_v, taps, decay.reshape(1, WIDTH), residual,
            gain.reshape(1, WIDTH), queries, keys,
        )

    inner = Mesh(mesh.devices.reshape(sizes), AXES)
    rows = ("zh", "y", "x")
    array = P(rows, "mp")
    return jax.shard_map(
        local, mesh=inner,
        in_specs=(array, array, array, P("mp", None), P("mp"), array, P("mp"), array, array),
        out_specs=(array, array), check_vma=False,
    )


def solution(mesh):
    seq, nm = mesh.shape["seq"], mesh.shape["mp"]
    return build(mesh, (2, seq // 8, 4, nm))
```

time: 604 us -> 99.3 us (0.16)
  the two profiles are of different devices: /device:TPU:1 before, /device:TPU:452 now
where the time goes in v1:
time: 99.3 us; the launch traced here: 99.2 us
  Pallas kernels  96.3 us (97%)
  local copies, waits for them, and re-layouts  2.26 us (2%)
    pallas_call x1, Pallas kernels, local(): pl.pallas_call(functools.partial(body, sizes), out_shape=(block, block),...  96.3 us
    unnamed x4, local copies, waits for them, and re-layouts  2.26 us

profile of v1, /device:TPU:452, one launch (start us, length us, event | category | flops | bytes accessed | tf_op | source)
XLA Modules:
  0.0 99.2 jit_solution(14359792664282246821)
XLA Ops:
  0.6 96.3 %shard_map.104 = (bf16[256,256]{1,0:T(8,128)(2,1)}, bf16[256,256]{1,0:T(8,128)(2,1)}) custom-call(bf16[256,256]{1,0:T(8,128)(2,1)} %sq_ref.1, bf16[256,256]{1,0:T(8,128)(2,1)} %sk_ref.1, bf16[256,256]{1,0:T(8,128)(2,1)} %sv_ref.1, f32[256,128]{1,0:T(8,128)} %taps_ref.1, f32[1,256]{1,0:T(1,128)} %bitcast.2, bf16[256,256]{1,0:T(8,128)(2,1)} %res_ref.1, ...), custom_call_target="tpu_custom_call" | custom-call | tf_op jit(solution)/shard_map/pallas_call | solution.py:297
  96.9 0.0 copy-start
  96.9 1.6 %copy.13 = bf16[256,256]{1,0:T(8,128)(2,1)} copy(bf16[256,256]{1,0:T(8,128)(2,1)} %get-tuple-element.4) | data formatting | bytes 262144
  98.5 0.0 copy-done
  98.5 0.7 copy.14
Async XLA Ops:
  96.9 1.6 %copy-start = (bf16[256,256]{1,0:T(8,128)(2,1)S(1)}, bf16[256,256]{1,0:T(8,128)(2,1)}, u32[]{:S(2)}) copy-start(bf16[256,256]{1,0:T(8,128)(2,1)} %get-tuple-element.5) | copy-start | bytes 393220

commit v2 on v1

--- a/solution.py
+++ b/solution.py
@@ -77,25 +77,47 @@
 
     sends = []
 
-    def spread(src, table, send, recv, first, slot):
-        for d in range(1, nx):
-            copy = remote(
-                src, table.at[slot], send.at[first + d], recv.at[slot],
-                at_x(lax.rem(x + d, nx)),
-            )
-            copy.start()
-            sends.append(copy)
+    left, right = lax.rem(x + nx - 1, nx), lax.rem(x + 1, nx)
+    halves = (pl.ds(0, ROWS // 2), pl.ds(ROWS // 2, ROWS // 2))
+
+    def spread(src, table, send, recv, half, act="start"):
+        slot = (zh if half == 0 else 1 - zh) * nx + x
+        for kind, target in ((0, right), (1, left)):
+            n = half * 4 + kind
+            copy = remote(src, table.at[slot], send.at[n], recv.at[n], at_x(target))
+            getattr(copy, act)()
+
+    def forward(table, send, recv, half, act="start"):
+        base = (zh if half == 0 else 1 - zh) * nx
+        for kind, target, column in ((0, right, left), (1, left, right)):
+            n = half * 4 + kind
+            piece = table.at[base + column]
+            if act == "start":
+                remote(piece, piece, send.at[n], recv.at[n], at_x(target)).wait_recv()
+            piece = piece.at[halves[kind]]
+            copy = remote(piece, piece, send.at[n + 2], recv.at[n + 2], at_x(target))
+            getattr(copy, act)()
+
+    def finish(table, send, recv, half):
+        far = (zh if half == 0 else 1 - zh) * nx + lax.rem(x + 2, nx)
+        for kind in range(2):
+            n = half * 4 + kind + 2
+            piece = table.at[far].at[halves[kind]]
+            remote(piece, piece, send.at[n], recv.at[n], at_x(left)).wait_recv()
 
     def across(src, table, send, recv):
-        copy = remote(src, table.at[mine], send.at[0], recv.at[mine], partner)
-        copy.start()
-        sends.append(copy)
-
-    def arrived(table, send, recv, slot):
-        remote(table.at[slot], table.at[slot], send.at[0], recv.at[slot], partner).wait_recv()
-
-    across(k_ref, k_all, k_send, k_recv)
-    spread(k_ref, k_all, k_send, k_recv, 0, mine)
+        return remote(src, table.at[mine], send.at[8], recv.at[8], partner)
+
+    def arrived(table, send, recv):
+        remote(table.at[other], table.at[other], send.at[8], recv.at[8], partner).wait_recv()
+
+    gathers = ((k_all, k_send, k_recv), (v_all, v_send, v_recv))
+
+    @pl.when(zh == 0)
+    def _():
+        across(k_ref, k_all, k_send, k_recv).start()
+
+    spread(k_ref, k_all, k_send, k_recv, 0)
     for d in range(1, ny):
         copy = remote(
             q_ref, q_all.at[y], q_send.at[d], q_recv.at[y], at_y(lax.rem(y + d, ny))
@@ -121,8 +143,7 @@
     for r in range(8):
         shifted[r, r : r + TAPS, :] = edge
 
-    arrived(k_all, k_send, k_recv, other)
-    spread(k_all.at[other], k_all, k_send, k_recv, nx - 1, other)
+    forward(k_all, k_send, k_recv, 0)
 
     chunk = 64
 
@@ -165,47 +186,61 @@
     inverse = lax.rsqrt(square / (nm * WIDTH) + EPS)
     inverse = jnp.concatenate([inverse] * 16, axis=0).T
     inverse = jnp.concatenate([inverse] * (WIDTH // 128), axis=1)
-    normed = (filtered[...] * inverse * gain_ref[...]).astype(jnp.bfloat16)
-    normed_ref[...] = normed
-    v_all[mine] = normed
-    across(v_all.at[mine], v_all, v_send, v_recv)
-    spread(v_all.at[mine], v_all, v_send, v_recv, 0, mine)
-    arrived(v_all, v_send, v_recv, other)
-    spread(v_all.at[other], v_all, v_send, v_recv, nx - 1, other)
+    scaled = filtered[...] * inverse * gain_ref[...]
+    v_all[mine] = scaled.T.astype(jnp.bfloat16)
+
+    @pl.when(zh == 0)
+    def _():
+        across(v_all.at[mine], v_all, v_send, v_recv).start()
+
+    spread(v_all.at[mine], v_all, v_send, v_recv, 0)
+    normed_ref[...] = scaled.astype(jnp.bfloat16)
+
+    @pl.when(zh == 1)
+    def _():
+        arrived(k_all, k_send, k_recv)
+        spread(k_all.at[other], k_all, k_send, k_recv, 1)
+
+    forward(v_all, v_send, v_recv, 0)
+
+    @pl.when(zh == 1)
+    def _():
+        forward(k_all, k_send, k_recv, 1)
+        arrived(v_all, v_send, v_recv)
+        spread(v_all.at[other], v_all, v_send, v_recv, 1)
+        forward(v_all, v_send, v_recv, 1)
+
     for d in range(1, ny):
         source = lax.rem(y + d, ny)
         remote(
             q_all.at[source], q_all.at[source], q_send.at[d], q_recv.at[source], at_y(source)
         ).wait_recv()
-    for d in range(1, nx):
-        column = lax.rem(x + d, nx)
-        for z in range(nz):
-            arrived(k_all, k_send, k_recv, z * nx + column)
-            arrived(v_all, v_send, v_recv, z * nx + column)
+    for gather in gathers:
+        finish(*gather, 0)
+
+    @pl.when(zh == 1)
+    def _():
+        for gather in gathers:
+            finish(*gather, 1)
 
     def tile(h, q_slot, slot, masked):
         lanes = slice(h * HD, (h + 1) * HD)
         score = lax.dot_general(
-            q_all[q_slot, :, lanes], k_all[slot, :, lanes], (((1,), (1,)), ((), ())),
+            k_all[slot, :, lanes], q_all[q_slot, :, lanes], (((1,), (1,)), ((), ())),
             preferred_element_type=jnp.float32,
         ) * SCALE2
         if masked:
-            row = lax.broadcasted_iota(jnp.int32, (ROWS, ROWS), 0)
-            col = lax.broadcasted_iota(jnp.int32, (ROWS, ROWS), 1)
-            score = jnp.where(col <= row, score, LOW)
+            key = lax.broadcasted_iota(jnp.int32, (ROWS, ROWS), 0)
+            query = lax.broadcasted_iota(jnp.int32, (ROWS, ROWS), 1)
+            score = jnp.where(key <= query, score, LOW)
         before = m_ref[h]
-        now = jnp.maximum(before, jnp.max(score, axis=1, keepdims=True))
+        now = jnp.maximum(before, jnp.max(score, axis=0, keepdims=True))
         m_ref[h] = now
-        weight = jnp.exp2(score - jnp.concatenate([now] * (ROWS // 128), axis=1))
-        if masked:
-            weight = jnp.where(col <= row, weight, 0.0)
+        weight = jnp.exp2(score - now)
         factor = jnp.exp2(before - now)
-        lane_sum = weight[:, :128]
-        for i in range(1, ROWS // 128):
-            lane_sum = lane_sum + weight[:, i * 128 : (i + 1) * 128]
-        l_ref[h] = l_ref[h] * factor + lane_sum
+        l_ref[h] = l_ref[h] * factor + jnp.sum(weight, axis=0, keepdims=True)
         acc_ref[h] = acc_ref[h] * factor + jnp.dot(
-            weight.astype(jnp.bfloat16), v_all[slot, :, lanes],
+            v_all[slot, lanes, :], weight.astype(jnp.bfloat16),
             preferred_element_type=jnp.float32,
         )
 
@@ -232,12 +267,12 @@
 
         logs = []
         for h in range(HEADS):
-            amount = jnp.sum(l_ref[h], axis=1, keepdims=True)
+            amount = l_ref[h]
             amount = jnp.where(amount > 0.0, amount, 1.0)
-            part[q_slot, :, h * HD : (h + 1) * HD] = (acc_ref[h] / amount).astype(jnp.bfloat16)
+            part[q_slot, :, h * HD : (h + 1) * HD] = (acc_ref[h] / amount).T.astype(jnp.bfloat16)
             logs.append(m_ref[h] + jnp.log2(amount))
-        lane = lax.broadcasted_iota(jnp.int32, (ROWS, 128), 1)
-        stat[q_slot] = jnp.where(lane == 0, logs[0], logs[1]).T[:8]
+        head = lax.broadcasted_iota(jnp.int32, (8, ROWS), 0)
+        stat[q_slot] = jnp.where(head == 0, logs[0], logs[1])
 
         @pl.when(jnp.logical_not(is_own))
         def _():
@@ -283,6 +318,18 @@
 
     for copy in sends:
         copy.wait_send()
+    for src, (table, send, recv) in zip((k_ref, v_all.at[mine]), gathers):
+        spread(src, table, send, recv, 0, "wait_send")
+        forward(table, send, recv, 0, "wait_send")
+
+        @pl.when(zh == 0)
+        def _():
+            across(src, table, send, recv).wait_send()
+
+        @pl.when(zh == 1)
+        def _():
+            spread(table.at[other], table, send, recv, 1, "wait_send")
+            forward(table, send, recv, 1, "wait_send")
 
 
 def build(mesh, sizes):
@@ -306,10 +353,10 @@
                 vmem((ny, ROWS, WIDTH), bf), vmem((group, ROWS, WIDTH), bf),
                 vmem((group, ROWS, WIDTH), bf), vmem((ny, ROWS, WIDTH), bf),
                 vmem((ny, ROWS, WIDTH), bf), vmem((ny, 8, ROWS), f32), vmem((ny, 8, ROWS), f32),
-                vmem((HEADS, ROWS, 128), f32), vmem((HEADS, ROWS, 128), f32),
-                vmem((HEADS, ROWS, HD), f32),
+                vmem((HEADS, 1, ROWS), f32), vmem((HEADS, 1, ROWS), f32),
+                vmem((HEADS, HD, ROWS), f32),
                 dma((2,)), dma((2,)), dma((nm,)), dma((nm,)), dma((ny,)), dma((ny,)),
-                dma((2 * nx,)), dma((group,)), dma((2 * nx,)), dma((group,)),
+                dma((9,)), dma((9,)), dma((9,)), dma((9,)),
                 dma((ny,)), dma((ny,)), dma((ny,)), dma((ny,)),
             ],
             compiler_params=pltpu.CompilerParams(

time: 99.3 us -> 95.7 us (0.964)
  the two profiles are of different devices: /device:TPU:452 before, /device:TPU:262 now
where the time goes in v2:
time: 95.7 us; the launch traced here: 95.5 us
  Pallas kernels  92.6 us (97%)
  local copies, waits for them, and re-layouts  2.26 us (2%)
    pallas_call x1, Pallas kernels, local(): pl.pallas_call(functools.partial(body, sizes), out_shape=(block, block),...  92.6 us
    unnamed x4, local copies, waits for them, and re-layouts  2.26 us

profile of v2, /device:TPU:262, one launch (start us, length us, event | category | flops | bytes accessed | tf_op | source)
XLA Modules:
  0.0 95.5 jit_solution(13905365811766886646)
XLA Ops:
  0.6 92.6 %shard_map.104 = (bf16[256,256]{1,0:T(8,128)(2,1)}, bf16[256,256]{1,0:T(8,128)(2,1)}) custom-call(bf16[256,256]{1,0:T(8,128)(2,1)} %sq_ref.1, bf16[256,256]{1,0:T(8,128)(2,1)} %sk_ref.1, bf16[256,256]{1,0:T(8,128)(2,1)} %sv_ref.1, f32[256,128]{1,0:T(8,128)} %taps_ref.1, f32[1,256]{1,0:T(1,128)} %bitcast.2, bf16[256,256]{1,0:T(8,128)(2,1)} %res_ref.1, ...), custom_call_target="tpu_custom_call" | custom-call | tf_op jit(solution)/shard_map/pallas_call | solution.py:344
  93.3 0.0 copy-start
  93.3 1.6 %copy.13 = bf16[256,256]{1,0:T(8,128)(2,1)} copy(bf16[256,256]{1,0:T(8,128)(2,1)} %get-tuple-element.4) | data formatting | bytes 262144
  94.9 0.0 copy-done
  94.9 0.7 copy.14
Async XLA Ops:
  93.3 1.6 %copy-start = (bf16[256,256]{1,0:T(8,128)(2,1)S(1)}, bf16[256,256]{1,0:T(8,128)(2,1)}, u32[]{:S(2)}) copy-start(bf16[256,256]{1,0:T(8,128)(2,1)} %get-tuple-element.5) | copy-start | bytes 393220

commit v3 on v2

--- a/solution.py
+++ b/solution.py
@@ -142,8 +142,6 @@
     edge = jnp.where(seq > 0, edge, 0.0)
     for r in range(8):
         shifted[r, r : r + TAPS, :] = edge
-
-    forward(k_all, k_send, k_recv, 0)
 
     chunk = 64
 
@@ -195,6 +193,7 @@
 
     spread(v_all.at[mine], v_all, v_send, v_recv, 0)
     normed_ref[...] = scaled.astype(jnp.bfloat16)
+    forward(k_all, k_send, k_recv, 0)
 
     @pl.when(zh == 1)
     def _():
@@ -223,26 +222,35 @@
         for gather in gathers:
             finish(*gather, 1)
 
-    def tile(h, q_slot, slot, masked):
+    def group(h, q_slot, base, masked):
         lanes = slice(h * HD, (h + 1) * HD)
-        score = lax.dot_general(
-            k_all[slot, :, lanes], q_all[q_slot, :, lanes], (((1,), (1,)), ((), ())),
-            preferred_element_type=jnp.float32,
-        ) * SCALE2
-        if masked:
-            key = lax.broadcasted_iota(jnp.int32, (ROWS, ROWS), 0)
-            query = lax.broadcasted_iota(jnp.int32, (ROWS, ROWS), 1)
-            score = jnp.where(key <= query, score, LOW)
+        query = q_all[q_slot, :, lanes]
+        scores = []
+        for c in range(nx):
+            score = lax.dot_general(
+                k_all[base + c, :, lanes], query, (((1,), (1,)), ((), ())),
+                preferred_element_type=jnp.float32,
+            )
+            if masked:
+                key_pos = lax.broadcasted_iota(jnp.int32, (ROWS, ROWS), 0) + c * ROWS
+                query_pos = lax.broadcasted_iota(jnp.int32, (ROWS, ROWS), 1) + x * ROWS
+                score = jnp.where(key_pos <= query_pos, score, LOW)
+            scores.append(score)
         before = m_ref[h]
-        now = jnp.maximum(before, jnp.max(score, axis=0, keepdims=True))
+        top = functools.reduce(jnp.maximum, scores)
+        now = jnp.maximum(before, jnp.max(top, axis=0, keepdims=True) * SCALE2)
         m_ref[h] = now
-        weight = jnp.exp2(score - now)
         factor = jnp.exp2(before - now)
-        l_ref[h] = l_ref[h] * factor + jnp.sum(weight, axis=0, keepdims=True)
-        acc_ref[h] = acc_ref[h] * factor + jnp.dot(
-            v_all[slot, lanes, :], weight.astype(jnp.bfloat16),
-            preferred_element_type=jnp.float32,
-        )
+        weights = [jnp.exp2(score * SCALE2 - now) for score in scores]
+        summed = functools.reduce(jnp.add, weights)
+        l_ref[h] = l_ref[h] * factor + jnp.sum(summed, axis=0, keepdims=True)
+        total = acc_ref[h] * factor
+        for c in range(nx):
+            total = total + jnp.dot(
+                v_all[base + c, lanes, :], weights[c].astype(jnp.bfloat16),
+                preferred_element_type=jnp.float32,
+            )
+        acc_ref[h] = total
 
     def query_block(i, _):
         q_slot = lax.rem(y + 1 + i, ny)
@@ -250,12 +258,11 @@
         m_ref[...] = jnp.full_like(m_ref, LOW)
         l_ref[...] = jnp.zeros_like(l_ref)
         acc_ref[...] = jnp.zeros_like(acc_ref)
-        inside = jnp.where(q_slot > y, nx, jnp.where(is_own, x, 0))
-        count = zh * nx + inside
-
-        def step(slot, carry):
+        count = zh + jnp.where(q_slot > y, 1, 0)
+
+        def step(i, carry):
             for h in range(HEADS):
-                tile(h, q_slot, slot, False)
+                group(h, q_slot, i * nx, False)
             return carry
 
         lax.fori_loop(0, count, step, 0)
@@ -263,7 +270,7 @@
         @pl.when(is_own)
         def _():
             for h in range(HEADS):
-                tile(h, q_slot, mine, True)
+                group(h, q_slot, zh * nx, True)
 
         logs = []
         for h in range(HEADS):

time: 95.7 us -> 82.5 us (0.86)
  the two profiles are of different devices: /device:TPU:262 before, /device:TPU:256 now
where the time goes in v3:
time: 82.5 us; the launch traced here: 82.3 us
  Pallas kernels  79.4 us (96%)
  local copies, waits for them, and re-layouts  2.26 us (3%)
    pallas_call x1, Pallas kernels, local(): pl.pallas_call(functools.partial(body, sizes), out_shape=(block, block),...  79.4 us
    unnamed x4, local copies, waits for them, and re-layouts  2.26 us

profile of v3, /device:TPU:256, one launch (start us, length us, event | category | flops | bytes accessed | tf_op | source)
XLA Modules:
  0.0 82.3 jit_solution(15536126666650169245)
XLA Ops:
  0.6 79.4 %shard_map.104 = (bf16[256,256]{1,0:T(8,128)(2,1)}, bf16[256,256]{1,0:T(8,128)(2,1)}) custom-call(bf16[256,256]{1,0:T(8,128)(2,1)} %sq_ref.1, bf16[256,256]{1,0:T(8,128)(2,1)} %sk_ref.1, bf16[256,256]{1,0:T(8,128)(2,1)} %sv_ref.1, f32[256,128]{1,0:T(8,128)} %taps_ref.1, f32[1,256]{1,0:T(1,128)} %bitcast.2, bf16[256,256]{1,0:T(8,128)(2,1)} %res_ref.1, ...), custom_call_target="tpu_custom_call" | custom-call | tf_op jit(solution)/shard_map/pallas_call | solution.py:351
  80.0 0.0 copy-start
  80.0 1.6 %copy.13 = bf16[256,256]{1,0:T(8,128)(2,1)} copy(bf16[256,256]{1,0:T(8,128)(2,1)} %get-tuple-element.4) | data formatting | bytes 262144
  81.6 0.0 copy-done
  81.7 0.7 copy.14
Async XLA Ops:
  80.0 1.6 %copy-start = (bf16[256,256]{1,0:T(8,128)(2,1)S(1)}, bf16[256,256]{1,0:T(8,128)(2,1)}, u32[]{:S(2)}) copy-start(bf16[256,256]{1,0:T(8,128)(2,1)} %get-tuple-element.5) | copy-start | bytes 393220

commit v4 on v3

--- a/solution.py
+++ b/solution.py
@@ -113,17 +113,6 @@
 
     gathers = ((k_all, k_send, k_recv), (v_all, v_send, v_recv))
 
-    @pl.when(zh == 0)
-    def _():
-        across(k_ref, k_all, k_send, k_recv).start()
-
-    spread(k_ref, k_all, k_send, k_recv, 0)
-    for d in range(1, ny):
-        copy = remote(
-            q_ref, q_all.at[y], q_send.at[d], q_recv.at[y], at_y(lax.rem(y + d, ny))
-        )
-        copy.start()
-        sends.append(copy)
     q_all[y] = q_ref[...]
     k_all[mine] = k_ref[...]
 
@@ -138,6 +127,17 @@
         shifted[r, TAPS + r : TAPS + r + ROWS, :] = own_gated
     for copy in halos:
         copy.wait()
+    @pl.when(zh == 0)
+    def _():
+        across(k_ref, k_all, k_send, k_recv).start()
+
+    spread(k_ref, k_all, k_send, k_recv, 0)
+    for d in range(1, ny):
+        copy = remote(
+            q_ref, q_all.at[y], q_send.at[d], q_recv.at[y], at_y(lax.rem(y + d, ny))
+        )
+        copy.start()
+        sends.append(copy)
     edge = gate(halo_k[...], halo_v[...])
     edge = jnp.where(seq > 0, edge, 0.0)
     for r in range(8):

time: 82.5 us -> 84 us (1.018)
  the two profiles are of different devices: /device:TPU:256 before, /device:TPU:1 now
where the time goes in v4:
time: 84 us; the launch traced here: 83.9 us
  Pallas kernels  81 us (96%)
  local copies, waits for them, and re-layouts  2.26 us (3%)
    pallas_call x1, Pallas kernels, local(): pl.pallas_call(functools.partial(body, sizes), out_shape=(block, block),...  81 us
    unnamed x4, local copies, waits for them, and re-layouts  2.26 us

profile of v4, /device:TPU:1, one launch (start us, length us, event | category | flops | bytes accessed | tf_op | source)
XLA Modules:
  0.0 83.9 jit_solution(3918468704512549090)
XLA Ops:
  0.6 81.0 %shard_map.104 = (bf16[256,256]{1,0:T(8,128)(2,1)}, bf16[256,256]{1,0:T(8,128)(2,1)}) custom-call(bf16[256,256]{1,0:T(8,128)(2,1)} %sq_ref.1, bf16[256,256]{1,0:T(8,128)(2,1)} %sk_ref.1, bf16[256,256]{1,0:T(8,128)(2,1)} %sv_ref.1, f32[256,128]{1,0:T(8,128)} %taps_ref.1, f32[1,256]{1,0:T(1,128)} %bitcast.2, bf16[256,256]{1,0:T(8,128)(2,1)} %res_ref.1, ...), custom_call_target="tpu_custom_call" | custom-call | tf_op jit(solution)/shard_map/pallas_call | solution.py:351
  81.6 0.0 copy-start
  81.6 1.6 %copy.13 = bf16[256,256]{1,0:T(8,128)(2,1)} copy(bf16[256,256]{1,0:T(8,128)(2,1)} %get-tuple-element.4) | data formatting | bytes 262144
  83.2 0.0 copy-done
  83.2 0.7 copy.14
Async XLA Ops:
  81.6 1.6 %copy-start = (bf16[256,256]{1,0:T(8,128)(2,1)S(1)}, bf16[256,256]{1,0:T(8,128)(2,1)}, u32[]{:S(2)}) copy-start(bf16[256,256]{1,0:T(8,128)(2,1)} %get-tuple-element.5) | copy-start | bytes 393220

commit v5 on v3

--- a/solution.py
+++ b/solution.py
@@ -253,7 +253,9 @@
         acc_ref[h] = total
 
     def query_block(i, _):
-        q_slot = lax.rem(y + 1 + i, ny)
+        away = (i + 1) // 2
+        away = jnp.where(lax.rem(i, 2) == 1, ny // 2 - away, ny // 2 + away)
+        q_slot = lax.rem(y + away, ny)
         is_own = i == ny - 1
         m_ref[...] = jnp.full_like(m_ref, LOW)
         l_ref[...] = jnp.zeros_like(l_ref)

time: 82.5 us -> 74.5 us (0.903)
  the two profiles are of different devices: /device:TPU:256 before, /device:TPU:264 now
where the time goes in v5:
time: 74.5 us; the launch traced here: 74.3 us
  Pallas kernels  71.4 us (96%)
  local copies, waits for them, and re-layouts  2.26 us (3%)
    pallas_call x1, Pallas kernels, local(): pl.pallas_call(functools.partial(body, sizes), out_shape=(block, block),...  71.4 us
    unnamed x4, local copies, waits for them, and re-layouts  2.26 us

profile of v5, /device:TPU:264, one launch (start us, length us, event | category | flops | bytes accessed | tf_op | source)
XLA Modules:
  0.0 74.3 jit_solution(6703403487031434170)
XLA Ops:
  0.6 71.4 %shard_map.104 = (bf16[256,256]{1,0:T(8,128)(2,1)}, bf16[256,256]{1,0:T(8,128)(2,1)}) custom-call(bf16[256,256]{1,0:T(8,128)(2,1)} %sq_ref.1, bf16[256,256]{1,0:T(8,128)(2,1)} %sk_ref.1, bf16[256,256]{1,0:T(8,128)(2,1)} %sv_ref.1, f32[256,128]{1,0:T(8,128)} %taps_ref.1, f32[1,256]{1,0:T(1,128)} %bitcast.2, bf16[256,256]{1,0:T(8,128)(2,1)} %res_ref.1, ...), custom_call_target="tpu_custom_call" | custom-call | tf_op jit(solution)/shard_map/pallas_call | solution.py:353
  72.1 0.0 copy-start
  72.1 1.6 %copy.13 = bf16[256,256]{1,0:T(8,128)(2,1)} copy(bf16[256,256]{1,0:T(8,128)(2,1)} %get-tuple-element.4) | data formatting | bytes 262144
  73.7 0.0 copy-done
  73.7 0.7 copy.14
Async XLA Ops:
  72.1 1.6 %copy-start = (bf16[256,256]{1,0:T(8,128)(2,1)S(1)}, bf16[256,256]{1,0:T(8,128)(2,1)}, u32[]{:S(2)}) copy-start(bf16[256,256]{1,0:T(8,128)(2,1)} %get-tuple-element.5) | copy-start | bytes 393220
